TPU v7x, 256 devices: a whole 4x4x8 slice. The times are simulated.
256 devices in a mesh: dp: 32 (over z_lo, y, x), tensor: 8 (over z_hi, core).
Axes of the slice: x: 4, y: 4, z: 8 (z_hi: 4, z_lo: 2; z = z_hi * 2 + z_lo), core: 2. Of those that a mesh axis runs over, the one named last changes fastest.
Arguments:
- rollout_rows: bfloat16 [16384, 4608], P(('dp', 'tensor')), may hold values from -6 to 6
- pack_dest: int32 [16384], P(('dp', 'tensor')), may hold values from 0 to 16383, as said below
- lengths: int32 [17], replicated, may hold values from 128 to 1536, as said below
- pattern: int32 [128, 128], P('dp'), may hold values from 0 to 1, as said below
- norm_gain: float32 [4608], replicated, may hold values from 0.1 to 1.9
- w_query: bfloat16 [4608, 2048], P(None, 'tensor'), may hold values from -0.1875 to 0.1875
- w_key: bfloat16 [4608, 1024], P(None, 'tensor'), may hold values from -0.1875 to 0.1875
- w_value: bfloat16 [4608, 1024], P(None, 'tensor'), may hold values from -0.09375 to 0.09375
- w_out: bfloat16 [2048, 4608], P('tensor'), may hold values from -0.125 to 0.125
- post_gain: float32 [4608], replicated, may hold values from 0.1 to 1.9
Outputs:
- layer_out: bfloat16 [16384, 4608], P(('dp', 'tensor'))
Inputs may be any that keep to these rules, and one draw needn't show every extreme that they name: `pack_dest`: a permutation of the pack rows; a rollout row goes to a pack row of the same tensor index, and the 64 rollout rows of one device go to each dp index exactly 2 at a time. `lengths`: all multiples of 128, summing to 16384; the prompt is shorter than 512. pattern[q, q] = 1; pattern[q, k] = 1 only where k <= q and key block k lies in the first 512 pack rows or in a dp shard at most 3 before query block q's shard.
All inputs are finite; a program needn't handle non-finite values.
Results may differ from a plain program's by a relative error of at most 0.017.
Values may be sent and summed in bfloat16 or wider, within the bound.
No kernel may reach another device: no remote copies, remote signals or barrier semaphores. Data moves between devices by JAX's collectives and lax.ppermute only.
A program may use at most 128 MiB of HBM per device.

v0:
```python
import jax
import jax.numpy as jnp
from jax import lax
from jax.sharding import PartitionSpec as P

HD = 128
BLK = 128
SOFT_CAP = 50.0
QUERY_SCALE = 1.0 / 12.0
ROPE_BASE = 10000.0
EPSILON = 1e-06


def positions(row_ids, lengths):
    bounds = jnp.cumsum(lengths)
    prompt = lengths[0]
    passed = (row_ids[:, None] >= bounds[None, :]).astype(jnp.int32)
    offset_start = jnp.sum(passed * lengths[None, :], axis=1)
    return jnp.where(row_ids < prompt, row_ids, prompt + row_ids - offset_start)


def rotate(values, angle_pos):
    half_width = values.shape[-1] // 2
    inverse_freq = jnp.power(
        ROPE_BASE, -(jnp.arange(half_width, dtype=jnp.float32) * 2.0) / values.shape[-1]
    )
    angles = angle_pos[:, None] * inverse_freq[None, :]
    cosine = jnp.cos(angles)[:, None, :]
    sine_part = jnp.sin(angles)[:, None, :]
    front_half = values[..., :half_width]
    back_half = values[..., half_width:]
    return jnp.concatenate(
        [front_half * cosine - back_half * sine_part, back_half * cosine + front_half * sine_part],
        axis=-1,
    )


def rms_scale(values, gain):
    return values * lax.rsqrt(jnp.mean(values * values, axis=-1, keepdims=True) + EPSILON) * gain


def attend(running, queries, key_value, pats, q_start, low_block, high_block):
    query_count = queries.shape[0]
    head_count = queries.shape[1]
    head_width = queries.shape[3]
    block_count = key_value.shape[0] // BLK
    key_blocks = key_value.reshape(block_count, BLK, 2, head_count, head_width)
    q_ids = q_start + jnp.arange(query_count, dtype=jnp.int32)

    def step(block_index, current):
        column = lax.dynamic_index_in_dim(
            pats, jnp.clip(block_index, 0, pats.shape[1] - 1), 1, keepdims=False
        )
        active = (block_index >= low_block) & (block_index < high_block) & jnp.any(column == 1)

        def compute(inner):
            weighted, totals = inner
            block_pair = lax.dynamic_index_in_dim(key_blocks, block_index, 0, keepdims=False)
            scores = (
                jnp.einsum(
                    "qhgd,khd->hgqk", queries, block_pair[:, 0], preferred_element_type=jnp.float32
                )
                * QUERY_SCALE
            )
            capped = SOFT_CAP * jnp.tanh(scores / SOFT_CAP)
            k_ids = block_index * BLK + jnp.arange(BLK, dtype=jnp.int32)
            allowed = (jnp.repeat(column, BLK) == 1)[:, None] & (k_ids[None, :] <= q_ids[:, None])
            weights = jnp.where(allowed, jnp.exp(capped), jnp.float32(0.0))
            rounded = weights.astype(jnp.bfloat16)
            weighted = weighted + jnp.einsum(
                "hgqk,khd->hgqd", rounded, block_pair[:, 1], preferred_element_type=jnp.float32
            )
            totals = totals + jnp.sum(weights, axis=-1)
            return (weighted, totals)

        return lax.cond(active, compute, lambda inner: inner, current)

    return lax.fori_loop(0, block_count, step, running)


def body(
    rollout_rows, pack_dest, lengths, pattern, norm_gain, w_query, w_key, w_value, w_out, post_gain
):
    tok_count = rollout_rows.shape[0]
    data_count = lax.axis_size("dp")
    tens_count = lax.axis_size("tensor")
    shard_len = tok_count * tens_count
    per_peer = tok_count // data_count
    target_dev = pack_dest // shard_len
    target_slot = pack_dest % tok_count
    order_ids = jnp.arange(tok_count, dtype=jnp.int32)
    before = (target_dev[:, None] == target_dev[None, :]) & (
        order_ids[None, :] < order_ids[:, None]
    )
    bucket_rank = jnp.sum(before.astype(jnp.int32), axis=1)
    send_pos = target_dev * per_peer + bucket_rank
    placer = order_ids[:, None] == send_pos[None, :]
    send_rows = jnp.dot(
        placer.astype(jnp.bfloat16), rollout_rows, preferred_element_type=jnp.float32
    ).astype(jnp.bfloat16)
    send_slots = jnp.sum(jnp.where(placer, target_slot[None, :], 0), axis=1)
    got_rows, got_slots = (
        lax.all_to_all(
            send_rows.reshape(data_count, per_peer, -1),
            "dp",
            split_axis=0,
            concat_axis=0,
            tiled=True,
        ),
        lax.all_to_all(
            send_slots.reshape(data_count, per_peer), "dp", split_axis=0, concat_axis=0, tiled=True
        ),
    )
    arrange = order_ids[:, None] == got_slots.reshape(tok_count)[None, :]
    packed = jnp.dot(
        arrange.astype(jnp.bfloat16),
        got_rows.reshape(tok_count, -1),
        preferred_element_type=jnp.float32,
    ).astype(jnp.bfloat16)
    normed = rms_scale(packed.astype(jnp.float32), norm_gain).astype(jnp.bfloat16)
    data_index = lax.axis_index("dp")
    base_row = data_index * shard_len
    query_cols = w_query.shape[1]
    pair_cols = w_key.shape[1]
    kv_heads = pair_cols // HD
    group_size = query_cols // HD // kv_heads
    portion = lax.all_gather(normed, "tensor", axis=0, tiled=True)
    row_ids = base_row + jnp.arange(portion.shape[0], dtype=jnp.int32)
    angle_pos = positions(row_ids, lengths).astype(jnp.float32)
    query_part = jnp.dot(portion, w_query, preferred_element_type=jnp.float32)
    key_part = jnp.dot(portion, w_key, preferred_element_type=jnp.float32)
    value_part = jnp.dot(portion, w_value, preferred_element_type=jnp.float32)
    query_part = rotate(query_part.reshape(-1, query_cols // HD, HD), angle_pos).reshape(
        -1, query_cols
    )
    key_part = rotate(key_part.reshape(-1, kv_heads, HD), angle_pos).reshape(-1, pair_cols)
    projected = jnp.concatenate([query_part, key_part, value_part], axis=1).astype(jnp.bfloat16)
    queries = projected[:, :query_cols].reshape(shard_len, kv_heads, group_size, HD)
    key_value = projected[:, query_cols:]
    block_total = pattern.shape[1]
    start_state = (
        jnp.zeros((kv_heads, group_size, shard_len, HD), jnp.float32),
        jnp.zeros((kv_heads, group_size, shard_len), jnp.float32),
    )
    weighted, totals = attend(
        start_state,
        queries,
        lax.all_gather(key_value, "dp", axis=0, tiled=True),
        pattern,
        base_row,
        0,
        block_total,
    )
    attended = weighted / totals[..., None]
    heads_out = (
        jnp.transpose(attended, (2, 0, 1, 3)).reshape(shard_len, query_cols).astype(jnp.bfloat16)
    )
    summed = lax.psum_scatter(
        jnp.dot(heads_out, w_out, preferred_element_type=jnp.float32).astype(jnp.bfloat16),
        "tensor",
        scatter_dimension=0,
        tiled=True,
    ).astype(jnp.float32)
    result = packed.astype(jnp.float32) + rms_scale(summed, post_gain)
    return result.astype(jnp.bfloat16)


def solution(mesh):
    placed = (
        P(("dp", "tensor"), None),
        P(("dp", "tensor")),
        P(),
        P("dp", None),
        P(),
        P(None, "tensor"),
        P(None, "tensor"),
        P(None, "tensor"),
        P("tensor", None),
        P(),
    )
    return jax.shard_map(
        body, mesh=mesh, in_specs=placed, out_specs=P(("dp", "tensor"), None), check_vma=False
    )
```

profile of v0, /device:TPU:65, one launch (start us, length us, event | category | flops | bytes accessed | tf_op | source)
XLA Modules:
  0.0 567.5 jit_solution(9726202630693829458)
XLA Ops:
  6.5 0.8 and_select_fusion
  8.4 8.4 %all-to-all-start = ((s32[32,1,2]{2,1,0:T(1,128)}), s32[32,1,2]{2,1,0:T(1,128)S(1)}, u32[]{:S(2)}, u32[]{:S(2)}) async-start(s32[32,1,2]{2,1,0:T(1,128)} %bitcast.12), calls=%async_computation | async-start | bytes 32768 | tf_op jit(solution)/shard_map/all_to_all | solution.py:110
  16.8 1.4 convolution_convert_fusion.2
  18.1 1.0 reshape.231
  19.2 4.6 all-to-all-done
  23.7 3.9 all-to-all-start.1
  29.0 8.0 %all-to-all-done.1 = bf16[32,2,4608]{2,1,0:T(2,128)(2,1)S(1)} async-done(((bf16[32,2,4608]{2,1,0:T(2,128)(2,1)}), bf16[32,2,4608]{2,1,0:T(2,128)(2,1)S(1)}, u32[]{:S(2)}, u32[]{:S(2)}) %all-to-all-start.1) | async-done | bytes 589856 | tf_op jit(solution)/shard_map/all_to_all | solution.py:103
  37.7 1.0 copy-done.2
  38.7 1.0 multiply_convert_fusion
  42.6 55.9 %all-gather.3.cloned.1.call-done = bf16[512,4608]{1,0:T(8,128)(2,1)} async-done(((bf16[64,4608]{1,0:T(8,128)(2,1)}), bf16[512,4608]{1,0:T(8,128)(2,1)}) %all-gather.3.cloned.1.call-update) | async-done | bytes 4718608 | tf_op jit(solution)/shard_map/all_gather | solution.py:127
  98.5 4.2 convolution_bitcast_fusion.1
  103.3 1.7 convolution_convert_fusion.3
  106.1 1.8 multiply_cosine_fusion
  107.9 4.5 fusion.30
  113.4 1.2 copy.42
  114.5 1.2 subtract_convert_fusion
  115.9 138.8 %all-gather.5.cloned.1.call-done = bf16[16384,256]{0,1:T(8,128)(2,1)} async-done(((bf16[512,256]{0,1:T(8,128)(2,1)}), bf16[16384,256]{0,1:T(8,128)(2,1)}) %all-gather.5.cloned.1.call-update) | async-done | bytes 8388624 | tf_op jit(solution)/shard_map/all_gather | solution.py:148
  254.7 9.2 %copy.43 = bf16[32,8,128,128]{3,2,1,0:T(8,128)(2,1)} copy(bf16[32,8,128,128]{3,1,2,0:T(8,128)(2,1)} %bitcast.70) | data formatting | bytes 16777216
  263.9 13.1 %copy.38 = bf16[128,128,2,1,128]{4,1,2,3,0:T(8,128)(2,1)} copy(bf16[128,128,2,1,128]{1,0,4,2,3:T(8,128)(2,1)} %bitcast.69) | data formatting | bytes 16777216
  277.0 178.3 %while.16 = (s32[]{:T(128)}, f32[1,2,512,128]{3,2,1,0:T(8,128)S(1)}, f32[1,2,512]{2,1,0:T(2,128)S(1)}, s32[4,128]{0,1:T(8,128)S(1)}, bf16[128,128,2,1,128]{4,1,2...) while((s32[]{:T(128)}, ...), condition=%wide.region_10.11_spmd.clone, body=%wide.region_5.10_spmd.clone.sunk | while | flops 68027032 | bytes 2189677 | solution.py:78
  278.3 1.7 conditional.3
  278.3 0.8 dynamic-slice_bitcast_fusion
  281.4 1.7 conditional.3
  281.4 0.8 dynamic-slice_bitcast_fusion
  284.4 1.7 conditional.3
  284.4 0.8 dynamic-slice_bitcast_fusion
  287.5 1.7 conditional.3
  287.5 0.8 dynamic-slice_bitcast_fusion
  455.5 3.5 convolution_convert_fusion
  459.1 98.5 %reduce-scatter.2.cloned.1.call-done = bf16[64,4608]{1,0:T(8,128)(2,1)} async-done(((bf16[512,4608]{1,0:T(8,128)(2,1)}), bf16[64,4608]{1,0:T(8,128)(2,1)}) %reduce-scatter.2.cloned.1.call-update) | async-done | bytes 589840 | tf_op jit(solution)/shard_map/reduce_scatter | solution.py:158
  557.6 1.3 fusion.12
  558.9 2.1 fusion.15
  (464 shorter events, 96.2 us)
Async XLA Ops:
  6.5 449.0 %copy-start = (bf16[256,4608]{1,0:T(8,128)(2,1)S(1)}, bf16[256,4608]{1,0:T(8,128)(2,1)}, u32[]{:S(2)}) copy-start(bf16[256,4608]{1,0:T(8,128)(2,1)} %param.22) | copy-start | bytes 7077892
  8.4 15.4 %all-to-all-start = ((s32[32,1,2]{2,1,0:T(1,128)}), s32[32,1,2]{2,1,0:T(1,128)S(1)}, u32[]{:S(2)}, u32[]{:S(2)}) async-start(s32[32,1,2]{2,1,0:T(1,128)} %bitcast.12), calls=%async_computation | async-start | bytes 32768 | tf_op jit(solution)/shard_map/all_to_all | solution.py:110
  23.7 13.3 %all-to-all-start.1 = ((bf16[32,2,4608]{2,1,0:T(2,128)(2,1)}), bf16[32,2,4608]{2,1,0:T(2,128)(2,1)S(1)}, u32[]{:S(2)}, u32[]{:S(2)}) async-start(bf16[32,2,4608]{2,1,0:T(2,128)(2,1)} %reshape.231), calls=%async_computation.1 | async-start | bytes 1179648 | tf_op jit(solution)/shard_map/all_to_all | solution.py:103
  27.6 70.9 %all-gather.3.cloned.1.call-start = ((), (), s32[]{:S(2)}) async-start(), calls=%async_computation.3 | async-start | bytes 5308416 | tf_op jit(solution)/shard_map/all_gather | solution.py:127
  37.3 1.4 copy-start.6
  37.7 1.0 copy-start.2
  38.7 1.1 copy-start.7
  38.7 59.8 %copy-start.4 = (bf16[4608,128]{1,0:T(8,128)(2,1)S(1)}, bf16[4608,128]{1,0:T(8,128)(2,1)}, u32[]{:S(2)}) copy-start(bf16[4608,128]{1,0:T(8,128)(2,1)} %param.20) | copy-start | bytes 3538948
  39.7 215.0 %all-gather.5.cloned.1.call-start = ((), (), s32[]{:S(2)}) async-start(), calls=%async_computation.4 | async-start | bytes 8650752 | tf_op jit(solution)/shard_map/all_gather | solution.py:148
  98.5 4.8 copy-start.1
  98.5 4.8 copy-start.5
  103.3 2.7 copy-start.8
  105.7 451.9 %reduce-scatter.2.cloned.1.call-start = ((), (), s32[]{:S(2)}) async-start(), calls=%async_computation.5 | async-start | bytes 5308416 | tf_op jit(solution)/shard_map/reduce_scatter | solution.py:158
  459.1 99.8 %copy-start.3 = (f32[64,4608]{1,0:T(8,128)S(1)}, f32[64,4608]{1,0:T(8,128)}, u32[]{:S(2)}) copy-start(f32[64,4608]{1,0:T(8,128)} %copy-done.2) | copy-start | bytes 3538948
Sparse Core Ops, SparseCore 0:
  39.9 58.5 all-gather.2
  105.9 148.7 all-gather.4
  459.2 98.3 reduce-scatter.1
where the time goes:
time: 570 us; the launch traced here: 568 us
  waiting for transfers between devices  306 us (54%)
  other arithmetic  95.4 us (17%)
  loops' own time  89.2 us (16%)
  local copies, waits for them, and re-layouts  33 us (6%)
  matrix products  18.1 us (3%)
  between operations  13.4 us (2%)
  starting transfers between devices  12.6 us (2%)
    all_gather x1, waiting for transfers between devices, body(): lax.all_gather(key_value, 'dp', axis=0, tiled=True)  139 us
    reduce_scatter x1, waiting for transfers between devices, body(): lax.psum_scatter(jnp.dot(heads_out, w_out, preferred_element_type=jnp.flo...  98.5 us
    another operation x1, loops' own time, attend(): return lax.fori_loop(0, block_count, step, running)  87.4 us
    reduce_or x128, other arithmetic, step(): jnp.any(column == 1)  82.1 us
    all_gather x1, waiting for transfers between devices, body(): portion = lax.all_gather(normed, 'tensor', axis=0, tiled=True)  55.9 us
    unnamed x23, local copies, waits for them, and re-layouts  24.8 us
  transfers between devices with their start and end apart: 5, of which 5 were waited for; matrix products, arithmetic and copies ran while one was open for 3% of the time, Pallas kernels for 0%

commit v1 on v0

--- a/solution.py
+++ b/solution.py
@@ -9,6 +9,13 @@
 QUERY_SCALE = 1.0 / 12.0
 ROPE_BASE = 10000.0
 EPSILON = 1e-06
+
+
+def exchange_gather(x, axis, dim):
+    n_dev = lax.axis_size(axis)
+    blocks = jnp.stack([x for _ in range(n_dev)])
+    blocks = lax.all_to_all(blocks, axis, split_axis=0, concat_axis=0)
+    return jnp.concatenate(blocks, axis=dim)
 
 
 def positions(row_ids, lengths):
@@ -143,13 +150,7 @@
         jnp.zeros((kv_heads, group_size, shard_len), jnp.float32),
     )
     weighted, totals = attend(
-        start_state,
-        queries,
-        lax.all_gather(key_value, "dp", axis=0, tiled=True),
-        pattern,
-        base_row,
-        0,
-        block_total,
+        start_state, queries, exchange_gather(key_value, "dp", 0), pattern, base_row, 0, block_total
     )
     attended = weighted / totals[..., None]
     heads_out = (

time: 570 us -> 560 us (0.982)
  waiting for transfers between devices: 306 us -> 267 us
  local copies, waits for them, and re-layouts: 33 us -> 53.3 us
  starting transfers between devices: 12.6 us -> 19.6 us
    all_gather x1 -> x0, waiting for transfers between devices: 139 us -> none  [body(): lax.all_gather(key_value, 'dp', axis=0, tiled=True)]
    all_to_all x0 -> x1, waiting for transfers between devices: none -> 118 us  [exchange_gather(): blocks = lax.all_to_all(blocks, axis, split_axis=0, concat_axis=0)]
    another operation x1 -> x3, local copies, waits for them, and re-layouts: 0.68 us -> 18.7 us  [the longest x1 13.9 us: attend(): key_blocks = key_value.reshape(block_count, BLK, 2, head_count, head_width)]
    reduce_scatter x1, waiting for transfers between devices: 98.5 us -> 80.7 us  [body(): lax.psum_scatter(jnp.dot(heads_out, w_out, preferred_element_type=jnp.flo...]
    all_to_all x0 -> x1, local copies, waits for them, and re-layouts: none -> 11.3 us  [exchange_gather(): blocks = lax.all_to_all(blocks, axis, split_axis=0, concat_axis=0)]
    unnamed x23 -> x20, local copies, waits for them, and re-layouts: 24.8 us -> 15.6 us
    all_to_all x0 -> x1, starting transfers between devices: none -> 7.07 us  [exchange_gather(): blocks = lax.all_to_all(blocks, axis, split_axis=0, concat_axis=0)]
where the time goes in v1:
time: 560 us; the launch traced here: 557 us
  waiting for transfers between devices  267 us (48%)
  other arithmetic  95.6 us (17%)
  loops' own time  89.2 us (16%)
  local copies, waits for them, and re-layouts  53.3 us (10%)
  starting transfers between devices  19.6 us (4%)
  matrix products  18.1 us (3%)
  between operations  13.7 us (2%)
    all_to_all x1, waiting for transfers between devices, exchange_gather(): blocks = lax.all_to_all(blocks, axis, split_axis=0, concat_axis=0)  118 us
    another operation x1, loops' own time, attend(): return lax.fori_loop(0, block_count, step, running)  87.3 us
    reduce_or x128, other arithmetic, step(): jnp.any(column == 1)  82.1 us
    reduce_scatter x1, waiting for transfers between devices, body(): lax.psum_scatter(jnp.dot(heads_out, w_out, preferred_element_type=jnp.flo...  80.7 us
    all_gather x1, waiting for transfers between devices, body(): portion = lax.all_gather(normed, 'tensor', axis=0, tiled=True)  55.6 us
    unnamed x20, local copies, waits for them, and re-layouts  15.6 us
    another operation x1, local copies, waits for them, and re-layouts, attend(): key_blocks = key_value.reshape(block_count, BLK, 2, head_count, head_width)  13.9 us
    all_to_all x1, local copies, waits for them, and re-layouts, exchange_gather(): blocks = lax.all_to_all(blocks, axis, split_axis=0, concat_axis=0)  11.3 us
  transfers between devices with their start and end apart: 5, of which 5 were waited for; matrix products, arithmetic and copies ran while one was open for 3% of the time, Pallas kernels for 0%

profile of v1, /device:TPU:65, one launch (start us, length us, event | category | flops | bytes accessed | tf_op | source)
XLA Modules:
  0.0 556.7 jit_solution(13762436295810427857)
XLA Ops:
  8.4 8.4 %all-to-all-start = ((s32[32,1,2]{2,1,0:T(1,128)}), s32[32,1,2]{2,1,0:T(1,128)S(1)}, u32[]{:S(2)}, u32[]{:S(2)}) async-start(s32[32,1,2]{2,1,0:T(1,128)} %bitcast.12), calls=%async_computation | async-start | bytes 32768 | tf_op jit(solution)/shard_map/all_to_all | solution.py:117
  16.8 1.4 convolution_convert_fusion.2
  18.1 1.0 reshape.230
  19.2 4.7 all-to-all-done
  23.9 3.9 all-to-all-start.1
  29.3 8.1 %all-to-all-done.1 = bf16[32,2,4608]{2,1,0:T(2,128)(2,1)S(1)} async-done(((bf16[32,2,4608]{2,1,0:T(2,128)(2,1)}), bf16[32,2,4608]{2,1,0:T(2,128)(2,1)S(1)}, u32[]{:S(2)}, u32[]{:S(2)}) %all-to-all-start.1) | async-done | bytes 589856 | tf_op jit(solution)/shard_map/all_to_all | solution.py:110
  38.1 1.1 copy-done.2
  39.2 1.7 multiply_convert_fusion
  43.9 55.6 %all-gather.2.cloned.1.call-done = bf16[512,4608]{1,0:T(8,128)(2,1)} async-done(((bf16[64,4608]{1,0:T(8,128)(2,1)}), bf16[512,4608]{1,0:T(8,128)(2,1)}) %all-gather.2.cloned.1.call-update) | async-done | bytes 4718608 | tf_op jit(solution)/shard_map/all_gather | solution.py:134
  99.5 4.2 convolution_bitcast_fusion.1
  104.2 1.7 convolution_convert_fusion.3
  106.0 4.2 stack.2
  110.1 7.1 %all-to-all-start.2 = ((bf16[32,512,256]{1,2,0:T(8,128)(2,1)}), bf16[32,512,256]{1,2,0:T(8,128)(2,1)}, u32[]{:S(2)}, u32[]{:S(2)}) async-start(bf16[32,512,256]{1,2,0:T(8,128)(2,1)} %stack.2), calls=%async_computation.2 | async-start | bytes 16777216 | tf_op jit(solution)/shard_map/all_to_all | solution.py:17
  117.6 1.8 multiply_cosine_fusion
  119.4 4.5 fusion.30
  124.9 1.1 copy.44
  126.0 1.2 subtract_convert_fusion
  127.4 118.0 %all-to-all-done.2 = bf16[32,512,256]{1,2,0:T(8,128)(2,1)} async-done(((bf16[32,512,256]{1,2,0:T(8,128)(2,1)}), bf16[32,512,256]{1,2,0:T(8,128)(2,1)}, u32[]{:S(2)}, u32[]{:S(2)}) %all-to-all-start.2) | async-done | bytes 8388640 | tf_op jit(solution)/shard_map/all_to_all | solution.py:17
  245.4 11.3 %copy.36 = bf16[32,512,256]{1,0,2:T(8,128)(2,1)} copy(bf16[32,512,256]{1,2,0:T(8,128)(2,1)} %all-to-all-done.2) | data formatting | bytes 16777216 | tf_op jit(solution)/shard_map/all_to_all | solution.py:17
  256.7 13.9 %reshape_reshape.3 = bf16[128,128,2,1,128]{1,0,4,2,3:T(8,128)(2,1)} reshape(bf16[32,512,256]{1,0,2:T(8,128)(2,1)} %copy.36) | data formatting | bytes 16777216 | tf_op jit(solution)/shard_map/reshape;reshape | solution.py:54
  270.6 13.1 %copy.40 = bf16[128,128,2,1,128]{4,1,2,3,0:T(8,128)(2,1)} copy(bf16[128,128,2,1,128]{1,0,4,2,3:T(8,128)(2,1)} %reshape_reshape.3) | data formatting | bytes 16777216
  283.7 178.2 %while.16 = (s32[]{:T(128)}, f32[1,2,512,128]{3,2,1,0:T(8,128)S(1)}, f32[1,2,512]{2,1,0:T(2,128)S(1)}, s32[4,128]{0,1:T(8,128)S(1)}, bf16[128,128,2,1,128]{4,1,2...) while((s32[]{:T(128)}, ...), condition=%wide.region_10.11_spmd.clone, body=%wide.region_5.10_spmd.clone.sunk | while | flops 68027032 | bytes 2189677 | solution.py:85
  285.0 1.7 conditional.3
  285.1 0.8 dynamic-slice_bitcast_fusion
  288.1 1.7 conditional.3
  288.1 0.8 dynamic-slice_bitcast_fusion
  291.2 1.7 conditional.3
  294.2 1.7 conditional.3
  462.2 3.5 convolution_convert_fusion
  465.8 80.7 %reduce-scatter.2.cloned.1.call-done = bf16[64,4608]{1,0:T(8,128)(2,1)} async-done(((bf16[512,4608]{1,0:T(8,128)(2,1)}), bf16[64,4608]{1,0:T(8,128)(2,1)}) %reduce-scatter.2.cloned.1.call-update) | async-done | bytes 589840 | tf_op jit(solution)/shard_map/reduce_scatter | solution.py:159
  546.5 1.3 fusion.12
  547.8 2.1 fusion.15
  (463 shorter events, 98.2 us)
Async XLA Ops:
  6.5 455.7 %copy-start = (bf16[256,4608]{1,0:T(8,128)(2,1)S(1)}, bf16[256,4608]{1,0:T(8,128)(2,1)}, u32[]{:S(2)}) copy-start(bf16[256,4608]{1,0:T(8,128)(2,1)} %param.22) | copy-start | bytes 7077892
  8.4 15.5 %all-to-all-start = ((s32[32,1,2]{2,1,0:T(1,128)}), s32[32,1,2]{2,1,0:T(1,128)S(1)}, u32[]{:S(2)}, u32[]{:S(2)}) async-start(s32[32,1,2]{2,1,0:T(1,128)} %bitcast.12), calls=%async_computation | async-start | bytes 32768 | tf_op jit(solution)/shard_map/all_to_all | solution.py:117
  23.9 13.5 %all-to-all-start.1 = ((bf16[32,2,4608]{2,1,0:T(2,128)(2,1)}), bf16[32,2,4608]{2,1,0:T(2,128)(2,1)S(1)}, u32[]{:S(2)}, u32[]{:S(2)}) async-start(bf16[32,2,4608]{2,1,0:T(2,128)(2,1)} %reshape.230), calls=%async_computation.1 | async-start | bytes 1179648 | tf_op jit(solution)/shard_map/all_to_all | solution.py:110
  27.8 71.7 %all-gather.2.cloned.1.call-start = ((), (), s32[]{:S(2)}) async-start(), calls=%async_computation.4 | async-start | bytes 5308416 | tf_op jit(solution)/shard_map/all_gather | solution.py:134
  37.6 3.3 copy-start.6
  38.0 1.1 copy-start.2
  38.1 61.4 %copy-start.4 = (bf16[4608,128]{1,0:T(8,128)(2,1)S(1)}, bf16[4608,128]{1,0:T(8,128)(2,1)}, u32[]{:S(2)}) copy-start(bf16[4608,128]{1,0:T(8,128)(2,1)} %param.20) | copy-start | bytes 3538948
  99.5 4.8 copy-start.1
  99.5 4.8 copy-start.5
  110.1 7.3 %copy-start.7 = (s32[4,128]{1,0:T(4,128)S(1)}, s32[4,128]{1,0:T(4,128)}, u32[]{:S(2)}) copy-start(s32[4,128]{1,0:T(4,128)} %param.17) | copy-start | bytes 6148
  110.1 135.3 %all-to-all-start.2 = ((bf16[32,512,256]{1,2,0:T(8,128)(2,1)}), bf16[32,512,256]{1,2,0:T(8,128)(2,1)}, u32[]{:S(2)}, u32[]{:S(2)}) async-start(bf16[32,512,256]{1,2,0:T(8,128)(2,1)} %stack.2), calls=%async_computation.2 | async-start | bytes 16777216 | tf_op jit(solution)/shard_map/all_to_all | solution.py:17
  117.2 429.3 %reduce-scatter.2.cloned.1.call-start = ((), (), s32[]{:S(2)}) async-start(), calls=%async_computation.5 | async-start | bytes 5308416 | tf_op jit(solution)/shard_map/reduce_scatter | solution.py:159
  465.7 82.0 %copy-start.3 = (f32[64,4608]{1,0:T(8,128)S(1)}, f32[64,4608]{1,0:T(8,128)}, u32[]{:S(2)}) copy-start(f32[64,4608]{1,0:T(8,128)} %copy-done.2) | copy-start | bytes 3538948
Sparse Core Ops, SparseCore 0:
  41.0 58.3 all-gather.1
  465.9 80.5 reduce-scatter.1
